TPU v7x, 32 devices: a whole 2x2x4 slice. The times are simulated.
32 devices in a mesh: tile: 8 (over y, x, core), member: 4 (over z).
Axes of the slice: x: 2, y: 2, z: 4, core: 2. Of those that a mesh axis runs over, the one named last changes fastest.
Arguments:
- hx: bfloat16 [512, 32768], P('member', 'tile'), may hold values from -6 to 6
- obs_value: bfloat16 [32768], P('tile'), may hold values from -8 to 8
- obs_rinv: bfloat16 [32768], P('tile'), may hold values from 0.29882812 to 4
- obs_index: int32 [32, 1024], P('tile'), may hold values from 512 to 5631, as said below
- loc_weight: float32 [32, 1024], P(('tile', 'member')), may hold values from 0.05 to 1
- state: bfloat16 [512, 131072], P('member', 'tile'), may hold values from -6 to 6
Outputs:
- analysis: bfloat16 [512, 131072], P('member', 'tile')
Inputs may be any that keep to these rules, and one draw needn't show every extreme that they name: `obs_index`: row p lists 1024 distinct positions in the pool of tile p // 4: positions 0 .. 1023 are the last 1024 observations of the tile before it, the next 4096 the tile's own, the last 1024 the first observations of the tile after it; the tiles form a closed band. All positions of a row lie within 2048 consecutive positions.
All inputs are finite; a program needn't handle non-finite values.
Results may differ from a plain program's by a relative error of at most 0.012.
The roundings to bfloat16 on the way count: a program that leaves them out, or rounds other values in their place, can miss the bound.
Values may be sent and summed in bfloat16 or wider, within the bound.
No kernel may reach another device: no remote copies, remote signals or barrier semaphores. Data moves between devices by JAX's collectives and lax.ppermute only.
A program may use at most 64 MiB of HBM per device.

v0:
```python
import jax
import jax.numpy as jnp
from jax import lax
from jax.sharding import PartitionSpec as P

LOC = 1024
NS_ITERS = 3


def with_halo(block, sides, width):
    for axis, dim in sides:
        count = lax.axis_size(axis)
        forward = [(i, i + 1) for i in range(count - 1)]
        forward.append((count - 1, 0))
        backward = [(target, source) for source, target in forward]
        low = lax.ppermute(
            lax.slice_in_dim(block, block.shape[dim] - width, None, axis=dim), axis, forward
        )
        high = lax.ppermute(lax.slice_in_dim(block, 0, width, axis=dim), axis, backward)
        block = jnp.concatenate([low, block, high], axis=dim)
    return block


def product_f32(left, right, dims):
    return lax.dot_general(
        left.astype(jnp.float32),
        right.astype(jnp.float32),
        (dims, ((), ())),
        precision=lax.Precision.HIGHEST,
        preferred_element_type=jnp.float32,
    )


def analysis(obs_block, obs_pair, loc_row):
    members = obs_block.shape[0]
    block_f = obs_block.astype(jnp.float32)
    obs_mean = jnp.mean(block_f, axis=0)
    obs_root = jnp.sqrt(obs_pair[1].astype(jnp.float32) * loc_row)
    scaled = ((block_f - obs_mean) * obs_root).astype(jnp.bfloat16)
    innovation = (obs_pair[0].astype(jnp.float32) - obs_mean) * obs_root
    gram_matrix = product_f32(scaled, scaled, ((1,), (1,)))
    identity = jnp.eye(members, dtype=jnp.float32)
    system = gram_matrix + (members - 1.0) * identity
    projection = jnp.dot(scaled.astype(jnp.float32), innovation, precision=lax.Precision.HIGHEST)
    norm_a = jnp.sqrt(jnp.sum(system * system))
    upper_iter = system / norm_a
    lower_iter = identity
    for sweep in range(NS_ITERS):
        upper_b = upper_iter.astype(jnp.bfloat16)
        lower_b = lower_iter.astype(jnp.bfloat16)
        product = product_f32(lower_b, upper_b, ((1,), (0,)))
        half_step = (1.5 * identity - 0.5 * product).astype(jnp.bfloat16)
        if sweep + 1 < NS_ITERS:
            upper_iter = product_f32(upper_b, half_step, ((1,), (0,)))
        lower_iter = product_f32(half_step, lower_b, ((1,), (0,)))
    invroot = lower_iter / jnp.sqrt(norm_a)
    inner_w = jnp.dot(invroot, projection, precision=lax.Precision.HIGHEST)
    mean_w = jnp.dot(invroot, inner_w, precision=lax.Precision.HIGHEST)
    transform = jnp.sqrt(members - 1.0) * invroot + mean_w[:, None]
    return transform.astype(jnp.bfloat16)


def transform_state(transform, state_block):
    block_f = state_block.astype(jnp.float32)
    state_mean = jnp.mean(block_f, axis=0)
    state_pert = (block_f - state_mean).astype(jnp.bfloat16)
    combined = product_f32(transform, state_pert, ((0,), (0,)))
    return (state_mean + combined).astype(jnp.bfloat16)


def on_device(hx, obs_value, obs_rinv, obs_index, loc_weight, state):
    ens_dev = hx.shape[0]
    member_pos = lax.axis_index("member")
    stacked = jnp.concatenate([hx, obs_value[None, :], obs_rinv[None, :]], axis=0)
    obs_pool = with_halo(stacked, (("tile", 1),), LOC)
    own_index = lax.dynamic_index_in_dim(obs_index, member_pos, 0, keepdims=False)
    obs_pair = jnp.take(obs_pool[ens_dev:], own_index, axis=1)
    picked = jnp.take(obs_pool[:ens_dev], obs_index, axis=1)
    received = lax.all_to_all(picked, "member", split_axis=1, concat_axis=0, tiled=True)
    obs_block = received[:, 0, :]
    transform = analysis(obs_block, obs_pair, loc_weight[0])
    group_count = obs_index.shape[0]
    state_split = state.reshape(ens_dev, group_count, state.shape[1] // group_count)
    updated = transform_state(
        transform,
        lax.all_to_all(state_split, "member", split_axis=1, concat_axis=0, tiled=True)[:, 0, :],
    )
    result = lax.all_to_all(updated[:, None, :], "member", split_axis=0, concat_axis=1, tiled=True)
    return result.reshape(ens_dev, state.shape[1])


def solution(mesh):
    in_specs = (
        P("member", "tile"),
        P("tile"),
        P("tile"),
        P("tile", None),
        P(("tile", "member"), None),
        P("member", "tile"),
    )
    out_specs = P("member", "tile")
    return jax.shard_map(
        on_device, mesh=mesh, in_specs=in_specs, out_specs=out_specs, check_vma=False
    )
```

profile of v0, /device:TPU:0, one launch (start us, length us, event | category | flops | bytes accessed | tf_op | source)
XLA Modules:
  0.0 328.8 jit_solution(2803960686868438312)
XLA Ops:
  0.0 1.6 copy.52
  1.6 1.3 broadcast_in_dim.44
  2.9 1.3 broadcast_in_dim.45
  4.6 0.5 collective-permute-start
  5.1 2.9 collective-permute-start.1
  8.1 9.8 %collective-permute-done = bf16[130,1024]{0,1:T(8,128)(2,1)S(1)} collective-permute-done((bf16[130,1024]{0,1:T(8,128)(2,1)S(1)}, bf16[130,1024]{0,1:T(8,128)(2,1)S(1)}, u32[]{:S(2)}, u32[]{:S(2)}) %collective-permute-start) | collective-permute-done | bytes 266272 | tf_op jit(solution)/shard_map/ppermute | solution.py:16
  17.9 1.5 collective-permute-done.1
  19.3 10.2 %pad_maximum_fusion = bf16[130,6144]{0,1:T(8,128)(2,1)S(1)} fusion(bf16[130,1024]{0,1:T(8,128)(2,1)S(1)} %collective-permute-done.1, bf16[1,4096]{0,1:T(8,128)(2,1)S(1)} %broadcast_in_dim.45, bf16[1,4096]{0,1:T(8,128)(2,1)S(1)} %broadcast_in_dim.44, bf16[128,4096]{0,1:T(8,128)(2,1)S(1)} %copy.52, bf16[130,1024]{0,1:T(8,128)(2,1)S(1)} %collective-permute-done), kind=kLoop, calls=%fused_computation.7 | loop fusion | flops 7987200 | bytes 3194880 | tf_op jit(solution)/shard_map/concatenate | solution.py:20
  29.5 1.7 copy-done
  31.3 12.1 %gather_fusion = bf16[4096,128]{1,0:T(8,128)(2,1)S(1)} fusion(bf16[128,6144]{0,1:T(8,128)(2,1)S(1)} %slice.28, s32[4096]{0:T(1024)S(1)} %bitcast_clamp_fusion), kind=kCustom, calls=%fused_computation | custom fusion | bytes 2113536 | tf_op jit(solution)/shard_map/jit(_take)/gather | solution.py:78
  43.5 0.5 copy.55
  44.0 1.1 select_bitcast_fusion
  45.1 4.9 %all-to-all-start.1 = ((bf16[128,4,1024]{2,0,1:T(8,128)(2,1)}), bf16[128,4,1024]{2,0,1:T(8,128)(2,1)S(1)}, u32[]{:S(2)}, u32[]{:S(2)}) async-start(bf16[128,4,1024]{2,0,1:T(8,128)(2,1)} %select_bitcast_fusion), calls=%async_computation.1 | async-start | bytes 2097152 | tf_op jit(solution)/shard_map/all_to_all | solution.py:79
  50.0 4.7 %copy.65 = bf16[16,4,8,4096]{3,2,0,1:T(8,128)(2,1)} copy(bf16[16,4,8,4096]{3,2,1,0:T(8,128)(2,1)} %bitcast.79) | data formatting | bytes 8388608 | tf_op jit(solution)/shard_map/reshape | solution.py:83
  54.7 22.0 %all-to-all-done.1 = bf16[128,4,1024]{2,0,1:T(8,128)(2,1)S(1)} async-done(((bf16[128,4,1024]{2,0,1:T(8,128)(2,1)}), bf16[128,4,1024]{2,0,1:T(8,128)(2,1)S(1)}, u32[]{:S(2)}, u32[]{:S(2)}) %all-to-all-start.1) | async-done | bytes 1048608 | tf_op jit(solution)/shard_map/all_to_all | solution.py:79
  76.7 5.2 %all-to-all-start = ((bf16[128,4,4096]{2,0,1:T(8,128)(2,1)}), bf16[128,4,4096]{2,0,1:T(8,128)(2,1)}, u32[]{:S(2)}, u32[]{:S(2)}) async-start(bf16[128,4,4096]{2,0,1:T(8,128)(2,1)} %bitcast.76), calls=%async_computation | async-start | bytes 8388608 | tf_op jit(solution)/shard_map/all_to_all | solution.py:86
  81.9 3.2 gather_fusion.1
  85.8 1.5 multiply_reduce_fusion
  88.8 0.9 convolution_bitcast_fusion.1
  92.4 1.0 convolution_bitcast_fusion
  93.4 1.0 fusion.19
  94.4 81.2 %all-to-all-done = bf16[128,4,4096]{2,0,1:T(8,128)(2,1)} async-done(((bf16[128,4,4096]{2,0,1:T(8,128)(2,1)}), bf16[128,4,4096]{2,0,1:T(8,128)(2,1)}, u32[]{:S(2)}, u32[]{:S(2)}) %all-to-all-start) | async-done | bytes 4194336 | tf_op jit(solution)/shard_map/all_to_all | solution.py:86
  175.6 3.2 convert_reduce_fusion.1
  178.8 3.1 fusion
  181.8 4.6 %fusion.1 = bf16[512,1,4096]{2,0,1:T(8,128)(2,1)} fusion(bf16[512,4096]{1,0:T(8,128)(2,1)S(1)} %fusion, f32[4096]{0:T(1024)S(1)} %broadcast_multiply_fusion, f32[512,512]{1,0:T(8,128)S(1)} %convolution_divide_fusion, f32[512]{0:T(512)S(1)} %bitcast.82), kind=kOutput, calls=%fused_computation.5 | convolution fusion | flops 2152464384 | bytes 9455616 | tf_op jit(solution)/shard_map/dot_general | solution.py:25
  186.9 6.6 %reduce.6 = bf16[512,4096]{1,0:T(8,128)(2,1)} reduce(bf16[512,1,4096]{2,0,1:T(8,128)(2,1)} %fusion.1, bf16[]{:T(256)} %broadcast.126), dimensions={1}, to_apply=%copy.57.reduce_sub_computation | reduce | bytes 8388610 | tf_op jit(solution)/shard_map/broadcast_in_dim | solution.py:88
  193.5 6.2 %reshape.136 = bf16[4,2,262144]{2,1,0:T(2,128)(2,1)} reshape(bf16[512,4096]{1,0:T(8,128)(2,1)} %reduce.6) | data formatting | bytes 8388608
  199.7 98.7 %all_to_all.33 = bf16[4,2,262144]{2,1,0:T(2,128)(2,1)} all-to-all(bf16[4,2,262144]{2,1,0:T(2,128)(2,1)} %reshape.136), channel_id=1, replica_groups=mesh['tile'=8,'member'=4] {'member'}, dimensions={0} | all-to-all | bytes 8388608 | tf_op jit(solution)/shard_map/all_to_all | solution.py:88
  298.5 7.4 %reshape.137 = bf16[512,1,4096]{2,1,0:T(2,128)(2,1)} reshape(bf16[4,2,262144]{2,1,0:T(2,128)(2,1)} %all_to_all.33) | data formatting | bytes 8388608
  305.9 10.1 %copy.60 = bf16[512,1,4096]{2,0,1:T(8,128)(2,1)} copy(bf16[512,1,4096]{2,1,0:T(2,128)(2,1)} %reshape.137) | data formatting | bytes 8388608
  316.1 6.3 %copy.58 = bf16[128,4,1,4096]{0,3,1,2:T(8,128)(2,1)} copy(bf16[128,4,1,4096]{3,0,1,2:T(8,128)(2,1)} %bitcast.75) | data formatting | bytes 8388608 | tf_op jit(solution)/shard_map/all_to_all | solution.py:88
  322.4 6.4 %copy.59 = bf16[128,16384]{1,0:T(8,128)(2,1)} copy(bf16[128,16384]{0,1:T(8,128)(2,1)} %bitcast.77) | data formatting | bytes 8388608 | tf_op jit(solution)/shard_map/reshape | solution.py:89
  (31 shorter events, 5.2 us)
Async XLA Ops:
  0.0 8.1 %copy-start.1 = (s32[4,1024]{1,0:T(4,128)S(1)}, s32[4,1024]{1,0:T(4,128)}, u32[]{:S(2)}) copy-start(s32[4,1024]{1,0:T(4,128)} %param.9) | copy-start | bytes 49156
  4.6 13.3 %collective-permute-start = (bf16[130,1024]{0,1:T(8,128)(2,1)S(1)}, bf16[130,1024]{0,1:T(8,128)(2,1)S(1)}, u32[]{:S(2)}, u32[]{:S(2)}) collective-permute-start(bf16[130,1024]{0,1:T(8,128)(2,1)S(1)} %get-tuple-element.7), channel_id=1, source_target_pairs={{0,4},{4,8},{8,12},{12,16},{16,20},{20,24},{24,28},{28,0},{1,5},{5... | collective-permute-start | bytes 798728 | tf_op jit(solution)/shard_map/ppermute | solution.py:16
  5.1 14.2 %collective-permute-start.1 = (bf16[130,1024]{0,1:T(8,128)(2,1)S(1)}, bf16[130,1024]{0,1:T(8,128)(2,1)S(1)}, u32[]{:S(2)}, u32[]{:S(2)}) collective-permute-start(bf16[130,1024]{0,1:T(8,128)(2,1)S(1)} %get-tuple-element.8), channel_id=1, source_target_pairs={{4,0},{8,4},{12,8},{16,12},{20,16},{24,20},{28,24},{0,28},{5,1},{9... | collective-permute-start | bytes 798728 | tf_op jit(solution)/shard_map/ppermute | solution.py:19
  29.5 1.7 copy-start
  45.1 31.6 %all-to-all-start.1 = ((bf16[128,4,1024]{2,0,1:T(8,128)(2,1)}), bf16[128,4,1024]{2,0,1:T(8,128)(2,1)S(1)}, u32[]{:S(2)}, u32[]{:S(2)}) async-start(bf16[128,4,1024]{2,0,1:T(8,128)(2,1)} %select_bitcast_fusion), calls=%async_computation.1 | async-start | bytes 2097152 | tf_op jit(solution)/shard_map/all_to_all | solution.py:79
  76.7 5.2 %slice-start = ((bf16[130,6144]{0,1:T(8,128)(2,1)}), bf16[2,6144]{0,1:T(8,128)(2,1)S(1)}, s32[]{:S(2)}) async-start(bf16[130,6144]{0,1:T(8,128)(2,1)} %copy-done), calls=%async_computation.3 | async-start | bytes 3145728 | tf_op jit(solution)/shard_map/slice | solution.py:77
  76.7 8.6 %copy-start.2 = (f32[1,1024]{1,0:T(1,128)S(1)}, f32[1,1024]{1,0:T(1,128)}, u32[]{:S(2)}) copy-start(f32[1,1024]{1,0:T(1,128)} %param.10) | copy-start | bytes 12292
  76.7 98.9 %all-to-all-start = ((bf16[128,4,4096]{2,0,1:T(8,128)(2,1)}), bf16[128,4,4096]{2,0,1:T(8,128)(2,1)}, u32[]{:S(2)}, u32[]{:S(2)}) async-start(bf16[128,4,4096]{2,0,1:T(8,128)(2,1)} %bitcast.76), calls=%async_computation | async-start | bytes 8388608 | tf_op jit(solution)/shard_map/all_to_all | solution.py:86
where the time goes:
time: 330 us; the launch traced here: 329 us
  waiting for transfers between devices  114 us (35%)
  blocking collectives  98.7 us (30%)
  local copies, waits for them, and re-layouts  63.7 us (19%)
  other arithmetic  25 us (8%)
  starting transfers between devices  13.6 us (4%)
  matrix products  12.4 us (4%)
    all_to_all x1, blocking collectives, on_device(): lax.all_to_all(updated[:, None, :], 'member', split_axis=0, concat_axis=1...  98.7 us
    all_to_all x1, waiting for transfers between devices, on_device(): lax.all_to_all(state_split, 'member', split_axis=1, concat_axis=0, tiled=...  81.2 us
    unnamed x10, local copies, waits for them, and re-layouts  27.1 us
    all_to_all x1, waiting for transfers between devices, on_device(): lax.all_to_all(picked, 'member', split_axis=1, concat_axis=0, tiled=True)  22 us
    gather x2, local copies, waits for them, and re-layouts, on_device(): picked = jnp.take(obs_pool[:ens_dev], obs_index, axis=1)  12.7 us
    concatenate x1, other arithmetic, with_halo(): block = jnp.concatenate([low, block, high], axis=dim)  10.2 us
    ppermute x1, waiting for transfers between devices, with_halo(): lax.ppermute(lax.slice_in_dim(block, block.shape[dim] - width, None, axis...  9.77 us
    dot_general x10, matrix products, product_f32(): lax.dot_general(left.astype(jnp.float32), right.astype(jnp.float32), (dim...  9.54 us
  transfers between devices with their start and end apart: 4, of which 4 were waited for; matrix products, arithmetic and copies ran while one was open for 5% of the time, Pallas kernels for 0%

commit v1 on v0

--- a/solution.py
+++ b/solution.py
@@ -5,6 +5,29 @@
 
 LOC = 1024
 NS_ITERS = 3
+
+
+def cut_along(shard, dim, size):
+    before, after = (shard.shape[:dim], shard.shape[dim + 1 :])
+    return jnp.moveaxis(shard.reshape(*before, size, -1, *after), dim, 0)
+
+
+def in_order(blocks, dim):
+    dims = list(blocks.shape[1:])
+    dims[dim] *= blocks.shape[0]
+    return jnp.moveaxis(blocks, 0, dim).reshape(dims)
+
+
+def exchange_directly(x, axis, split_dim, concat_dim):
+    count, index = (lax.axis_size(axis), lax.axis_index(axis))
+    pieces = cut_along(x, split_dim, count)
+    out = pieces
+    for hop in range(1, count):
+        target, source = ((index + hop) % count, (index - hop) % count)
+        sent = lax.dynamic_index_in_dim(pieces, target, 0)
+        other = lax.ppermute(sent, axis, [(i, (i + hop) % count) for i in range(count)])
+        out = lax.dynamic_update_slice_in_dim(out, other, source, axis=0)
+    return in_order(out, concat_dim)
 
 
 def with_halo(block, sides, width):
@@ -81,10 +104,7 @@
     transform = analysis(obs_block, obs_pair, loc_weight[0])
     group_count = obs_index.shape[0]
     state_split = state.reshape(ens_dev, group_count, state.shape[1] // group_count)
-    updated = transform_state(
-        transform,
-        lax.all_to_all(state_split, "member", split_axis=1, concat_axis=0, tiled=True)[:, 0, :],
-    )
+    updated = transform_state(transform, exchange_directly(state_split, "member", 1, 0)[:, 0, :])
     result = lax.all_to_all(updated[:, None, :], "member", split_axis=0, concat_axis=1, tiled=True)
     return result.reshape(ens_dev, state.shape[1])
 

time: 330 us -> 294 us (0.89)
  waiting for transfers between devices: 114 us -> 51.1 us
  local copies, waits for them, and re-layouts: 63.7 us -> 82.2 us
  blocking collectives: 98.7 us -> 105 us
    all_to_all x1 -> x0, waiting for transfers between devices: 81.2 us -> none  [on_device(): lax.all_to_all(state_split, 'member', split_axis=1, concat_axis=0, tiled=...]
    ppermute x0 -> x3, waiting for transfers between devices: none -> 13.7 us  [exchange_directly(): lax.ppermute(sent, axis, [(i, (i + hop) % count) for i in range(count)])]
    ppermute x1, waiting for transfers between devices: 1.46 us -> 12.3 us  [with_halo(): lax.ppermute(lax.slice_in_dim(block, 0, width, axis=dim), axis, backward)]
    ppermute x1, waiting for transfers between devices: 9.77 us -> 1.98 us  [with_halo(): lax.ppermute(lax.slice_in_dim(block, block.shape[dim] - width, None, axis...]
    convert_element_type x0 -> x1, local copies, waits for them, and re-layouts: none -> 7.07 us  [transform_state(): block_f = state_block.astype(jnp.float32)]
    ppermute x0 -> x3, starting transfers between devices: none -> 6.99 us  [exchange_directly(): lax.ppermute(sent, axis, [(i, (i + hop) % count) for i in range(count)])]
    dynamic_update_slice x0 -> x3, local copies, waits for them, and re-layouts: none -> 6.79 us  [exchange_directly(): out = lax.dynamic_update_slice_in_dim(out, other, source, axis=0)]
    unnamed x10 -> x19, local copies, waits for them, and re-layouts: 27.1 us -> 33.4 us
  transfers between devices with their start and end apart: 4 -> 6, of which waited for: 4 -> 4; matrix products, arithmetic and copies ran while one was open for 5% -> 18% of each run, Pallas kernels for 0% -> 0%
where the time goes in v1:
time: 294 us; the launch traced here: 293 us
  blocking collectives  105 us (36%)
  local copies, waits for them, and re-layouts  82.2 us (28%)
  waiting for transfers between devices  51.1 us (17%)
  other arithmetic  27.4 us (9%)
  matrix products  14.6 us (5%)
  starting transfers between devices  11.6 us (4%)
    all_to_all x1, blocking collectives, on_device(): lax.all_to_all(updated[:, None, :], 'member', split_axis=0, concat_axis=1...  105 us
    unnamed x19, local copies, waits for them, and re-layouts  33.4 us
    all_to_all x1, waiting for transfers between devices, on_device(): lax.all_to_all(picked, 'member', split_axis=1, concat_axis=0, tiled=True)  23.1 us
    ppermute x3, waiting for transfers between devices, exchange_directly(): lax.ppermute(sent, axis, [(i, (i + hop) % count) for i in range(count)])  13.7 us
    gather x2, local copies, waits for them, and re-layouts, on_device(): picked = jnp.take(obs_pool[:ens_dev], obs_index, axis=1)  13.4 us
    ppermute x1, waiting for transfers between devices, with_halo(): lax.ppermute(lax.slice_in_dim(block, 0, width, axis=dim), axis, backward)  12.3 us
    dot_general x10, matrix products, product_f32(): lax.dot_general(left.astype(jnp.float32), right.astype(jnp.float32), (dim...  11.7 us
    concatenate x1, other arithmetic, with_halo(): block = jnp.concatenate([low, block, high], axis=dim)  7.29 us
  transfers between devices with their start and end apart: 6, of which 4 were waited for; matrix products, arithmetic and copies ran while one was open for 18% of the time, Pallas kernels for 0%

profile of v1, /device:TPU:0, one launch (start us, length us, event | category | flops | bytes accessed | tf_op | source)
XLA Modules:
  0.0 292.9 jit_solution(14597237844249492118)
XLA Ops:
  0.0 6.4 %copy.87 = bf16[128,16384]{0,1:T(8,128)(2,1)} copy(bf16[128,16384]{1,0:T(8,128)(2,1)} %param.11) | data formatting | bytes 8388608 | tf_op args[5]
  6.4 3.6 %dynamic-slice_bitcast_fusion = (bf16[1,128,1,4096]{1,3,0,2:T(8,128)(2,1)}, bf16[1,128,1,4096]{1,3,0,2:T(8,128)(2,1)}, bf16[1,128,1,4096]{1,3,0,2:T(8,128)(2,1)}) fusion(bf16[128,4,1,4096]{0,3,1,2:T(8,128)(2,1)} %bitcast.82, s32[]{:T(128)S(6)} %select_n.88, s32[]{:T(128)S(6)} %select_n.84, s32[]{:T(128)S(6)} %select_n.80), kind=kLoop, calls=%fused_computation.36 | loop fusion | bytes 6291468 | tf_op jit(solution)/shard_map/jit(dynamic_index_in_dim)/dynamic_slice | solution.py:27
  10.0 3.1 %collective-permute-start = (bf16[1,128,1,4096]{1,3,0,2:T(8,128)(2,1)}, bf16[1,128,1,4096]{1,3,0,2:T(8,128)(2,1)}, u32[]{:S(2)}, u32[]{:S(2)}) collective-permute-start(bf16[1,128,1,4096]{1,3,0,2:T(8,128)(2,1)} %get-tuple-element.9), channel_id=1, source_target_pairs={{0,1},{1,2},{2,3},{3,0},{4,5},{5,6},{6,7},{7,4},{8,9},{9,10},{10,1... | collective-permute-start | bytes 3145736 | tf_op jit(solution)/shard_map/ppermute | solution.py:28
  13.0 2.6 collective-permute-start.1
  15.6 1.3 collective-permute-start.2
  18.2 1.6 copy.94
  22.3 12.3 %collective-permute-done.4 = bf16[130,1024]{0,1:T(8,128)(2,1)} collective-permute-done((bf16[130,1024]{0,1:T(8,128)(2,1)}, bf16[130,1024]{0,1:T(8,128)(2,1)}, u32[]{:S(2)}, u32[]{:S(2)}) %collective-permute-start.4) | collective-permute-done | bytes 266272 | tf_op jit(solution)/shard_map/ppermute | solution.py:42
  34.7 2.0 collective-permute-done.3
  36.7 7.3 %pad_maximum_fusion = bf16[130,6144]{0,1:T(8,128)(2,1)S(1)} fusion(bf16[130,1024]{0,1:T(8,128)(2,1)} %collective-permute-done.4, bf16[1,4096]{0,1:T(8,128)(2,1)S(1)} %broadcast_in_dim.45, bf16[1,4096]{0,1:T(8,128)(2,1)S(1)} %broadcast_in_dim.44, bf16[128,4096]{0,1:T(8,128)(2,1)S(1)} %copy.94, bf16[130,1024]{0,1:T(8,128)(2,1)} %collective-permute-done.3), kind=kLoop, calls=%fused_computation.6 | loop fusion | flops 7987200 | bytes 3194880 | tf_op jit(solution)/shard_map/concatenate | solution.py:43
  44.0 1.6 copy-done.1
  45.7 12.1 %gather_fusion = bf16[4096,128]{1,0:T(8,128)(2,1)S(1)} fusion(bf16[128,6144]{0,1:T(8,128)(2,1)S(1)} %slice.28, s32[4096]{0:T(1024)S(1)} %bitcast_clamp_fusion), kind=kCustom, calls=%fused_computation | custom fusion | bytes 2113536 | tf_op jit(solution)/shard_map/jit(_take)/gather | solution.py:101
  59.2 2.4 select_bitcast_fusion
  61.6 3.5 %all-to-all-start = ((bf16[128,4,1024]{2,0,1:T(8,128)(2,1)}), bf16[128,4,1024]{2,0,1:T(8,128)(2,1)S(1)}, u32[]{:S(2)}, u32[]{:S(2)}) async-start(bf16[128,4,1024]{2,0,1:T(8,128)(2,1)} %select_bitcast_fusion), calls=%async_computation | async-start | bytes 2097152 | tf_op jit(solution)/shard_map/all_to_all | solution.py:102
  65.1 3.2 %gather_fusion.1 = bf16[1024,2]{1,0:T(8,128)(2,1)S(1)} fusion(bf16[2,6144]{0,1:T(8,128)(2,1)S(1)} %slice-done, s32[1024]{0:T(1024)S(1)} %broadcast_clamp_fusion), kind=kCustom, calls=%fused_computation.1 | custom fusion | bytes 12288 | tf_op jit(solution)/shard_map/jit(_take)/gather | solution.py:100
  68.5 2.3 constant_dynamic-update-slice_fusion.2
  70.8 13.7 %collective-permute-done.1 = bf16[1,128,1,4096]{1,3,0,2:T(8,128)(2,1)} collective-permute-done((bf16[1,128,1,4096]{1,3,0,2:T(8,128)(2,1)}, bf16[1,128,1,4096]{1,3,0,2:T(8,128)(2,1)}, u32[]{:S(2)}, u32[]{:S(2)}) %collective-permute-start.1) | collective-permute-done | bytes 1048608 | tf_op jit(solution)/shard_map/ppermute | solution.py:28
  84.5 2.3 constant_dynamic-update-slice_fusion.1
  86.8 2.3 constant_dynamic-update-slice_fusion
  89.1 2.8 convert_reduce_fusion.1
  91.9 7.1 %copy.99 = f32[4,128,1,4096]{3,1,0,2:T(8,128)} copy(bf16[4,128,1,4096]{1,3,0,2:T(8,128)(2,1)} %constant_dynamic-update-slice_fusion) | data formatting | bytes 12582912 | tf_op jit(solution)/shard_map/convert_element_type | solution.py:87
  99.0 6.4 %fusion = bf16[512,4096]{1,0:T(8,128)(2,1)} fusion(f32[4,128,1,4096]{3,1,0,2:T(8,128)} %copy.99, f32[4096]{0:T(1024)S(1)} %broadcast_multiply_fusion), kind=kLoop, calls=%fused_computation.3 | loop fusion | flops 4194304 | bytes 12599296 | tf_op jit(solution)/shard_map/convert_element_type | solution.py:89
  105.3 23.1 %all-to-all-done = bf16[128,4,1024]{2,0,1:T(8,128)(2,1)S(1)} async-done(((bf16[128,4,1024]{2,0,1:T(8,128)(2,1)}), bf16[128,4,1024]{2,0,1:T(8,128)(2,1)S(1)}, u32[]{:S(2)}, u32[]{:S(2)}) %all-to-all-start) | async-done | bytes 1048608 | tf_op jit(solution)/shard_map/all_to_all | solution.py:102
  128.9 2.3 multiply_reduce_fusion
  131.9 1.8 fusion.5
  139.7 4.6 %fusion.1 = bf16[512,1,4096]{2,0,1:T(8,128)(2,1)} fusion(bf16[512,4096]{1,0:T(8,128)(2,1)S(1)} %copy-done, f32[4096]{0:T(1024)S(1)} %broadcast_multiply_fusion, f32[512,512]{1,0:T(8,128)S(1)} %convolution_divide_fusion, f32[512]{0:T(512)S(1)} %bitcast.89), kind=kOutput, calls=%fused_computation.5 | convolution fusion | flops 2152464384 | bytes 9455616 | tf_op jit(solution)/shard_map/dot_general | solution.py:48
  144.8 6.7 %reduce.4 = bf16[512,4096]{1,0:T(8,128)(2,1)} reduce(bf16[512,1,4096]{2,0,1:T(8,128)(2,1)} %fusion.1, bf16[]{:T(256)} %broadcast.132), dimensions={1}, to_apply=%copy.100.reduce_sub_computation | reduce | bytes 8388610 | tf_op jit(solution)/shard_map/broadcast_in_dim | solution.py:108
  151.5 6.2 %reshape.130 = bf16[4,2,262144]{2,1,0:T(2,128)(2,1)} reshape(bf16[512,4096]{1,0:T(8,128)(2,1)} %reduce.4) | data formatting | bytes 8388608
  157.7 104.9 %all_to_all.24 = bf16[4,2,262144]{2,1,0:T(2,128)(2,1)} all-to-all(bf16[4,2,262144]{2,1,0:T(2,128)(2,1)} %reshape.130), channel_id=1, replica_groups=mesh['tile'=8,'member'=4] {'member'}, dimensions={0} | all-to-all | bytes 8388608 | tf_op jit(solution)/shard_map/all_to_all | solution.py:108
  262.7 7.4 %reshape.131 = bf16[512,1,4096]{2,1,0:T(2,128)(2,1)} reshape(bf16[4,2,262144]{2,1,0:T(2,128)(2,1)} %all_to_all.24) | data formatting | bytes 8388608
  270.1 10.1 %copy.109 = bf16[512,1,4096]{2,0,1:T(8,128)(2,1)} copy(bf16[512,1,4096]{2,1,0:T(2,128)(2,1)} %reshape.131) | data formatting | bytes 8388608
  280.2 6.3 %copy.101 = bf16[128,4,1,4096]{0,3,1,2:T(8,128)(2,1)} copy(bf16[128,4,1,4096]{3,0,1,2:T(8,128)(2,1)} %bitcast.84) | data formatting | bytes 8388608 | tf_op jit(solution)/shard_map/all_to_all | solution.py:108
  286.6 6.4 %copy.102 = bf16[128,16384]{1,0:T(8,128)(2,1)} copy(bf16[128,16384]{0,1:T(8,128)(2,1)} %bitcast.85) | data formatting | bytes 8388608 | tf_op jit(solution)/shard_map/reshape | solution.py:109
  (48 shorter events, 12.2 us)
Async XLA Ops:
  6.4 10.6 %copy-start.3 = (bf16[4096]{0:T(1024)(128)(2,1)S(1)}, bf16[4096]{0:T(1024)(128)(2,1)}, u32[]{:S(2)}) copy-start(bf16[4096]{0:T(1024)(128)(2,1)} %param.8) | copy-start | bytes 24580
  6.4 11.2 %copy-start.4 = (bf16[4096]{0:T(1024)(128)(2,1)S(1)}, bf16[4096]{0:T(1024)(128)(2,1)}, u32[]{:S(2)}) copy-start(bf16[4096]{0:T(1024)(128)(2,1)} %param.7) | copy-start | bytes 24580
  10.0 58.5 %collective-permute-start = (bf16[1,128,1,4096]{1,3,0,2:T(8,128)(2,1)}, bf16[1,128,1,4096]{1,3,0,2:T(8,128)(2,1)}, u32[]{:S(2)}, u32[]{:S(2)}) collective-permute-start(bf16[1,128,1,4096]{1,3,0,2:T(8,128)(2,1)} %get-tuple-element.9), channel_id=1, source_target_pairs={{0,1},{1,2},{2,3},{3,0},{4,5},{5,6},{6,7},{7,4},{8,9},{9,10},{10,1... | collective-permute-start | bytes 3145736 | tf_op jit(solution)/shard_map/ppermute | solution.py:28
  13.0 71.5 %collective-permute-start.1 = (bf16[1,128,1,4096]{1,3,0,2:T(8,128)(2,1)}, bf16[1,128,1,4096]{1,3,0,2:T(8,128)(2,1)}, u32[]{:S(2)}, u32[]{:S(2)}) collective-permute-start(bf16[1,128,1,4096]{1,3,0,2:T(8,128)(2,1)} %get-tuple-element.8), channel_id=1, source_target_pairs={{0,2},{1,3},{2,0},{3,1},{4,6},{5,7},{6,4},{7,5},{8,10},{9,11},{10,... | collective-permute-start | bytes 3145736 | tf_op jit(solution)/shard_map/ppermute | solution.py:28
  15.6 6.6 %copy-start.2 = (s32[4,1024]{1,0:T(4,128)S(1)}, s32[4,1024]{1,0:T(4,128)}, u32[]{:S(2)}) copy-start(s32[4,1024]{1,0:T(4,128)} %param.9) | copy-start | bytes 49156
  15.6 71.2 %collective-permute-start.2 = (bf16[1,128,1,4096]{1,3,0,2:T(8,128)(2,1)}, bf16[1,128,1,4096]{1,3,0,2:T(8,128)(2,1)}, u32[]{:S(2)}, u32[]{:S(2)}) collective-permute-start(bf16[1,128,1,4096]{1,3,0,2:T(8,128)(2,1)} %get-tuple-element.7), channel_id=1, source_target_pairs={{0,3},{1,0},{2,1},{3,2},{4,7},{5,4},{6,5},{7,6},{8,11},{9,8},{10,9... | collective-permute-start | bytes 3145736 | tf_op jit(solution)/shard_map/ppermute | solution.py:28
  21.1 13.6 %collective-permute-start.4 = (bf16[130,1024]{0,1:T(8,128)(2,1)}, bf16[130,1024]{0,1:T(8,128)(2,1)}, u32[]{:S(2)}, u32[]{:S(2)}) collective-permute-start(bf16[130,1024]{0,1:T(8,128)(2,1)} %get-tuple-element.11), channel_id=1, source_target_pairs={{4,0},{8,4},{12,8},{16,12},{20,16},{24,20},{28,24},{0,28},{5,1},{9... | collective-permute-start | bytes 798728 | tf_op jit(solution)/shard_map/ppermute | solution.py:42
  22.2 14.5 %collective-permute-start.3 = (bf16[130,1024]{0,1:T(8,128)(2,1)}, bf16[130,1024]{0,1:T(8,128)(2,1)}, u32[]{:S(2)}, u32[]{:S(2)}) collective-permute-start(bf16[130,1024]{0,1:T(8,128)(2,1)} %get-tuple-element.10), channel_id=1, source_target_pairs={{0,4},{4,8},{8,12},{12,16},{16,20},{20,24},{24,28},{28,0},{1,5},{5... | collective-permute-start | bytes 798728 | tf_op jit(solution)/shard_map/ppermute | solution.py:39
  44.0 1.6 copy-start.1
  59.2 5.9 %slice-start = ((bf16[130,6144]{0,1:T(8,128)(2,1)}), bf16[2,6144]{0,1:T(8,128)(2,1)S(1)}, s32[]{:S(2)}) async-start(bf16[130,6144]{0,1:T(8,128)(2,1)} %copy-done.1), calls=%async_computation.2 | async-start | bytes 3145728 | tf_op jit(solution)/shard_map/slice | solution.py:100
  59.2 9.3 %copy-start.5 = (f32[1,1024]{1,0:T(1,128)S(1)}, f32[1,1024]{1,0:T(1,128)}, u32[]{:S(2)}) copy-start(f32[1,1024]{1,0:T(1,128)} %param.10) | copy-start | bytes 12292
  61.6 66.8 %all-to-all-start = ((bf16[128,4,1024]{2,0,1:T(8,128)(2,1)}), bf16[128,4,1024]{2,0,1:T(8,128)(2,1)S(1)}, u32[]{:S(2)}, u32[]{:S(2)}) async-start(bf16[128,4,1024]{2,0,1:T(8,128)(2,1)} %select_bitcast_fusion), calls=%async_computation | async-start | bytes 2097152 | tf_op jit(solution)/shard_map/all_to_all | solution.py:102
  131.9 2.2 copy-start.6
  136.8 2.9 copy-start
